TPU v7x, 32 devices: a whole 2x2x4 slice. The times are simulated.
32 devices in a mesh: cam: 4 (over y, x), dev: 8 (over z, core).
Axes of the slice: x: 2, y: 2, z: 4, core: 2. Of those that a mesh axis runs over, the one named last changes fastest.
Arguments:
- params: float32 [256, 59, 128], P('dev'), may hold values from -4 to 4
- moment_first: float32 [8, 4, 8, 59, 128], P('dev', 'cam'), may hold values from -3 to 3
- moment_second: float32 [8, 4, 8, 59, 128], P('dev', 'cam'), may hold values from 0.01 to 1
- cam_proj: float32 [8, 9, 59], P('cam'), may hold values from -0.75 to 0.75
- send_block: int32 [8, 8, 8, 2], P('cam', 'dev'), may hold values from 0 to 31
- tile_slot: int32 [8, 16, 8], P('cam', 'dev'), may hold values from 0 to 15, as said below
- tile_count: int32 [8, 16], P('cam', 'dev'), may hold values from 2 to 8, as said below
- targets: float32 [8, 16, 3, 256], P('cam', 'dev'), may hold values from 0 to 1
- split_block: int32 [8, 8], P('dev'), may hold values from 0 to 31, as said below
- split_live: int32 [8, 8], P('dev'), may hold values from 0 to 1, as said below
Outputs:
- images: float32 [8, 16, 3, 256], P('cam', 'dev')
- new_params: float32 [256, 59, 128], P('dev')
- new_first: float32 [8, 4, 8, 59, 128], P('dev', 'cam')
- new_second: float32 [8, 4, 8, 59, 128], P('dev', 'cam')
- children: float32 [64, 2, 59, 128], P('dev')
Inputs may be any that keep to these rules, and one draw needn't show every extreme that they name: `tile_count`: in every camera some tile has exactly 8 live entries. `tile_slot`: the entries of one tile's list are distinct; entries at positions from the tile's count on are not read. `split_block`: among an owner's entries where split_live is 1 the blocks are distinct. `split_live`: each row holds exactly 2 ones; in every draw some new owner has a one in every row.
All inputs are finite; a program needn't handle non-finite values.
Results may differ from a plain program's by a relative error of at most 0.0003.
Values sent between devices are 32-bit elements; how exact they have to be, the bound alone decides.
A program may use at most 64 MiB of HBM per device.

v0:
```python
import functools
import math

import jax
import jax.numpy as jnp
from jax import lax
from jax.experimental import pallas as pl
from jax.experimental.pallas import tpu as pltpu
from jax.sharding import PartitionSpec as P

TSIDE = 16
PROJ = 9
PAIR = 2
LOSS_WEIGHT = 256.0
RATE = 0.01
BETA_FIRST = 0.9
BETA_SECOND = 0.999
EPSILON = 1e-08
SHRINK = math.log(1.6)
LOG2E = math.log2(math.e)
MESH = pl.DeviceIdType.MESH
HIGHEST = lax.Precision.HIGHEST
F32 = jnp.float32
BF16 = jnp.bfloat16
VMEM = pl.BlockSpec(memory_space=pltpu.VMEM)
SMEM = pl.BlockSpec(memory_space=pltpu.SMEM)
BIG = 60 * 1024 * 1024


def split2(value):
    high = value.astype(BF16)
    return high, (value - high.astype(F32)).astype(BF16)


def dot32(left, right, dims=(((1,), (0,)), ((), ()))):
    return lax.dot_general(left, right, dims, preferred_element_type=F32)


def softplus(value):
    return jnp.maximum(value, 0.0) + jnp.log(1.0 + jnp.exp(-jnp.abs(value)))


def sigmoid(value):
    return 1.0 / (1.0 + jnp.exp(-value))


def project_kernel(
    send_ref, matrix_ref, params_ref, out_ref, rows_ref, parcels, land, send_sems, recv_sems
):
    values, owned, _ = params_ref.shape
    cameras, _, cap, owners = send_ref.shape
    me = lax.axis_index("dev")
    barrier = pltpu.get_barrier_semaphore()
    for step in range(1, owners):
        pl.semaphore_signal(
            barrier, inc=1, device_id={"dev": lax.rem(me + step, owners)}, device_id_type=MESH
        )
    matrix = matrix_ref[:, :values]
    for block in range(owned):
        rows_ref[block] = jnp.dot(
            matrix, params_ref[:, block, :], precision=HIGHEST, preferred_element_type=F32
        )
    for owner in range(owners):
        for camera in range(cameras):
            for place in range(cap):
                chosen = send_ref[camera, 0, place, owner]
                first = (camera * cap + place) * PROJ
                parcels[owner, first : first + PROJ, :] = rows_ref[
                    chosen, camera * 16 : camera * 16 + PROJ, :
                ]
    pl.semaphore_wait(barrier, owners - 1)
    copies = []
    for step in range(1, owners):
        peer = lax.rem(me + step, owners)
        copy = pltpu.make_async_remote_copy(
            src_ref=parcels.at[peer],
            dst_ref=land.at[me],
            send_sem=send_sems.at[step - 1],
            recv_sem=recv_sems.at[step - 1],
            device_id={"dev": peer},
            device_id_type=MESH,
        )
        copy.start()
        copies.append(copy)
    out_ref[me] = parcels[me]
    for step in range(1, owners):
        copies[step - 1].wait_recv()
        source = lax.rem(me - step + owners, owners)
        out_ref[source] = land[source]
    for copy in copies:
        copy.wait_send()


def project(send_block, matrix, params):
    cameras, _, cap, owners = send_block.shape
    values, owned, splats = params.shape
    shape = (owners, cameras * cap * PROJ, splats)
    return pl.pallas_call(
        project_kernel,
        out_shape=jax.ShapeDtypeStruct(shape, F32),
        in_specs=[SMEM, VMEM, VMEM],
        out_specs=VMEM,
        scratch_shapes=[
            pltpu.VMEM((owned, matrix.shape[0], splats), F32),
            pltpu.VMEM(shape, F32),
            pltpu.VMEM(shape, F32),
            pltpu.SemaphoreType.DMA((owners - 1,)),
            pltpu.SemaphoreType.DMA((owners - 1,)),
        ],
        compiler_params=pltpu.CompilerParams(
            collective_id=5, has_side_effects=True, vmem_limit_bytes=BIG
        ),
        name="project",
    )(send_block, matrix, params)


def exchange_kernel(axis, count, x_ref, out_ref, land, send_sems, recv_sems):
    me = lax.axis_index(axis)
    barrier = pltpu.get_barrier_semaphore()
    for step in range(1, count):
        pl.semaphore_signal(
            barrier, inc=1, device_id={axis: lax.rem(me + step, count)}, device_id_type=MESH
        )
    pl.semaphore_wait(barrier, count - 1)
    copies = []
    for step in range(1, count):
        peer = lax.rem(me + step, count)
        copy = pltpu.make_async_remote_copy(
            src_ref=x_ref.at[peer],
            dst_ref=land.at[me],
            send_sem=send_sems.at[step - 1],
            recv_sem=recv_sems.at[step - 1],
            device_id={axis: peer},
            device_id_type=MESH,
        )
        copy.start()
        copies.append(copy)
    out_ref[me] = x_ref[me]
    for step in range(1, count):
        copies[step - 1].wait_recv()
        source = lax.rem(me - step + count, count)
        out_ref[source] = land[source]
    for copy in copies:
        copy.wait_send()


def exchange(x, axis, ident):
    count = x.shape[0]
    return pl.pallas_call(
        functools.partial(exchange_kernel, axis, count),
        out_shape=jax.ShapeDtypeStruct(x.shape, F32),
        in_specs=[VMEM],
        out_specs=VMEM,
        scratch_shapes=[
            pltpu.VMEM(x.shape, F32),
            pltpu.SemaphoreType.DMA((count - 1,)),
            pltpu.SemaphoreType.DMA((count - 1,)),
        ],
        compiler_params=pltpu.CompilerParams(
            collective_id=ident, has_side_effects=True, vmem_limit_bytes=BIG
        ),
        name=f"exchange_{ident}",
    )(x)


def return_kernel(owners, groups, x_ref, out_ref, land, zsend, zrecv, csend, crecv):
    me = lax.axis_index("dev")
    group = lax.axis_index("cam")
    barrier = pltpu.get_barrier_semaphore()
    for step in range(1, owners):
        pl.semaphore_signal(
            barrier, inc=1, device_id={"dev": lax.rem(me + step, owners)}, device_id_type=MESH
        )
    for step in range(1, groups):
        pl.semaphore_signal(
            barrier, inc=1, device_id={"cam": lax.rem(group + step, groups)}, device_id_type=MESH
        )
    pl.semaphore_wait(barrier, owners + groups - 2)
    along = []
    for step in range(1, owners):
        peer = lax.rem(me + step, owners)
        copy = pltpu.make_async_remote_copy(
            src_ref=x_ref.at[peer],
            dst_ref=land.at[0, me],
            send_sem=zsend.at[step - 1],
            recv_sem=zrecv.at[step - 1],
            device_id={"dev": peer},
            device_id_type=MESH,
        )
        copy.start()
        along.append(copy)
    across = []
    for step in range(owners):
        source = lax.rem(me - step + owners, owners)
        if step:
            along[step - 1].wait_recv()
        piece = land.at[0, source] if step else x_ref.at[me]
        for turn in range(1, groups):
            copy = pltpu.make_async_remote_copy(
                src_ref=piece,
                dst_ref=land.at[turn, source],
                send_sem=csend.at[turn - 1, step],
                recv_sem=crecv.at[turn - 1, step],
                device_id={"cam": lax.rem(group - turn + groups, groups)},
                device_id_type=MESH,
            )
            copy.start()
            across.append((turn, source, copy))
        out_ref[0, source] = land[0, source] if step else x_ref[me]
    for turn, source, copy in across:
        copy.wait_recv()
        out_ref[turn, source] = land[turn, source]
    for copy in along:
        copy.wait_send()
    for _, _, copy in across:
        copy.wait_send()


def return_home(x, groups):
    owners = x.shape[0]
    shape = (groups,) + x.shape
    return pl.pallas_call(
        functools.partial(return_kernel, owners, groups),
        out_shape=jax.ShapeDtypeStruct(shape, F32),
        in_specs=[VMEM],
        out_specs=VMEM,
        scratch_shapes=[
            pltpu.VMEM(shape, F32),
            pltpu.SemaphoreType.DMA((owners - 1,)),
            pltpu.SemaphoreType.DMA((owners - 1,)),
            pltpu.SemaphoreType.DMA((groups - 1, owners)),
            pltpu.SemaphoreType.DMA((groups - 1, owners)),
        ],
        compiler_params=pltpu.CompilerParams(
            collective_id=7, has_side_effects=True, vmem_limit_bytes=BIG
        ),
        name="return_home",
    )(x)


def shape_of(raw):
    turn_x = jnp.tanh(raw[0])
    turn_y = jnp.tanh(raw[1])
    conic_a = 0.02 + 0.1 * softplus(raw[2])
    conic_c = 0.02 + 0.1 * softplus(raw[4])
    turn_b = jnp.tanh(raw[3])
    root = jnp.sqrt(conic_a * conic_c)
    return turn_x, turn_y, conic_a, conic_c, turn_b, root


def render_kernel(
    slot_ref, count_ref, received_ref, target_ref, image_ref, back_ref,
    feats, grads, weights, pairs, ratios, carry, before, after_tri, cot_rows, cot_cols, picture,
):
    cameras, tiles, _ = slot_ref.shape
    owners, rows, splats = received_ref.shape
    cap = rows // (PROJ * cameras)
    centre = 0.5 * TSIDE
    spread = 0.375 * TSIDE
    pixels = TSIDE * TSIDE
    half = 128
    per_chunk = half // TSIDE

    feats[...] = jnp.zeros(feats.shape, F32)
    grads[...] = jnp.zeros(grads.shape, F32)
    for index in range(cameras * cap):
        raw = [received_ref[:, index * PROJ + k, :] for k in range(PROJ)]
        turn_x, turn_y, conic_a, conic_c, turn_b, root = shape_of(raw)
        conic_b = 0.9 * root * turn_b
        feats[:, index, 0, :] = centre + spread * turn_x
        feats[:, index, 1, :] = centre + spread * turn_y
        feats[:, index, 2, :] = (0.5 * LOG2E) * conic_a
        feats[:, index, 3, :] = LOG2E * conic_b
        feats[:, index, 4, :] = (0.5 * LOG2E) * conic_c
        feats[:, index, 5, :] = math.log2(0.99) - LOG2E * softplus(6.0 - raw[5])
        for k in range(3):
            feats[:, index, 8 + k, :] = sigmoid(raw[6 + k])

    row = lax.broadcasted_iota(jnp.int32, (splats, splats), 0)
    column = lax.broadcasted_iota(jnp.int32, (splats, splats), 1)
    ones = jnp.ones((splats, splats), BF16)
    lower = jnp.where(row < column, 1.0, 0.0).astype(BF16)
    upper = jnp.where(row > column, 1.0, 0.0).astype(BF16)
    for part in range(2):
        before[part * splats : (part + 1) * splats, :splats] = lower
        before[part * splats : (part + 1) * splats, splats:] = ones
        after_tri[part * splats : (part + 1) * splats, :splats] = upper
        after_tri[part * splats : (part + 1) * splats, splats:] = ones
    grid = lax.broadcasted_iota(jnp.int32, (TSIDE, splats), 0).astype(F32) + 0.5
    pad_rows = jnp.zeros((8, splats), F32)

    def entry_of(camera, tile, position):
        slot = slot_ref[camera, tile, position]
        return slot // cap, camera * cap + slot % cap

    def tile_step(number, _):
        camera = number // tiles
        tile = number % tiles
        live = count_ref[camera, tile]
        carry[...] = jnp.zeros(carry.shape, F32)
        picture[...] = jnp.zeros(picture.shape, F32)

        def forward(pair, _):
            places = [PAIR * pair + sub for sub in range(PAIR)]
            alphas, logs, sums, shades = [], [], [], []
            for place in places:
                owner, index = entry_of(camera, tile, jnp.minimum(place, live - 1))
                part = lambda k: feats[owner, index, k : k + 1, :]
                off_x = grid - part(0)
                off_y = grid - part(1)
                in_x = -(part(2) * off_x * off_x)
                cross = -(part(3) * off_x)
                faint = jnp.where(place < live, part(5), -1e30)
                in_y = faint - part(4) * off_y * off_y
                for chunk in range(pixels // half):
                    lines = []
                    for line in range(chunk * per_chunk, (chunk + 1) * per_chunk):
                        lines.append(
                            in_x + (in_y[line : line + 1] + cross * off_y[line : line + 1])
                        )
                    alpha = jnp.exp2(jnp.concatenate(lines, axis=0))
                    log_keep = jnp.log2(1.0 - alpha)
                    alphas.append(alpha)
                    logs.append(log_keep)
                    sums.append(dot32(jnp.concatenate(split2(log_keep), axis=1), before[...]))
                colour_high, colour_low = split2(feats[owner, index, 8:16, :])
                colour_high = colour_high.astype(F32)
                colour_low = colour_low.astype(F32)
                shades.append(
                    jnp.concatenate(
                        [
                            jnp.concatenate([colour_high, colour_low], axis=0),
                            jnp.concatenate([colour_high, pad_rows], axis=0),
                        ],
                        axis=1,
                    ).astype(BF16)
                )
            chunks = pixels // half
            for chunk in range(chunks):
                where = slice(chunk * half, (chunk + 1) * half)
                held = carry[where, :]
                drawn = jnp.zeros((16, half), F32)
                for sub, place in enumerate(places):
                    at = sub * chunks + chunk
                    weight = alphas[at] * jnp.exp2(sums[at][:, :splats] + held)
                    held = held + sums[at][:, splats:]
                    both = jnp.concatenate(split2(weight), axis=1)
                    weights[place, where, :] = weight
                    pairs[place, where, :] = both
                    ratios[place, where, :] = alphas[at] * jnp.exp2(-logs[at])
                    drawn += dot32(shades[sub], both, (((1,), (1,)), ((), ())))
                carry[where, :] = held
                picture[:, where] += drawn[:8] + drawn[8:]
            return 0

        steps = (live + PAIR - 1) // PAIR
        lax.fori_loop(0, steps, forward, 0)
        for k in range(3):
            colour = picture[k : k + 1, :]
            image_ref[camera, k, pl.ds(tile, 1), :] = colour
            picture[k : k + 1, :] = LOSS_WEIGHT * (
                colour - target_ref[camera, k, pl.ds(tile, 1), :]
            )
        cot_high, cot_low = split2(picture[...])
        cot_high = cot_high.astype(F32)
        cot_low = cot_low.astype(F32)
        cot_rows[...] = jnp.concatenate([cot_high, cot_low], axis=0).astype(BF16)
        stacked = jnp.concatenate(
            [cot_high, cot_low, cot_high, jnp.zeros((half - 24, pixels), F32)], axis=0
        )
        cot_cols[...] = stacked.T.astype(BF16)
        carry[...] = jnp.zeros(carry.shape, F32)

        def backward(reverse, _):
            places = [PAIR * (steps - 1 - reverse) + PAIR - 1 - sub for sub in range(PAIR)]
            chunks = pixels // half
            spots, offsets, shaded, sums = [], [], [], []
            for place in places:
                owner, index = entry_of(camera, tile, jnp.minimum(place, live - 1))
                spots.append((owner, index))
                offsets.append(
                    (grid - feats[owner, index, 0:1, :], grid - feats[owner, index, 1:2, :])
                )
                colour_high, colour_low = split2(feats[owner, index, 8:16, :])
                colour_high = colour_high.astype(F32)
                shades = jnp.concatenate(
                    [
                        colour_high,
                        colour_high,
                        colour_low.astype(F32),
                        jnp.zeros((half - 24, splats), F32),
                    ],
                    axis=0,
                ).astype(BF16)
                for chunk in range(chunks):
                    where = slice(chunk * half, (chunk + 1) * half)
                    piece = dot32(cot_cols[where, :], shades) * weights[place, where, :]
                    shaded.append(piece)
                    sums.append(dot32(jnp.concatenate(split2(piece), axis=1), after_tri[...]))
            totals = [[jnp.zeros((TSIDE, splats), F32)] * 3 for _ in places]
            for chunk in range(chunks):
                where = slice(chunk * half, (chunk + 1) * half)
                held = carry[where, :]
                for sub, place in enumerate(places):
                    at = sub * chunks + chunk
                    pull = shaded[at] - (sums[at][:, :splats] + held) * ratios[place, where, :]
                    held = held + sums[at][:, splats:]
                    total0, total1, total2 = totals[sub]
                    off_y = offsets[sub][1]
                    for line in range(per_chunk):
                        height = off_y[chunk * per_chunk + line : chunk * per_chunk + line + 1]
                        piece = pull[line * TSIDE : (line + 1) * TSIDE]
                        lifted = piece * height
                        total0 += piece
                        total1 += lifted
                        total2 += lifted * height
                    totals[sub] = [total0, total1, total2]
                carry[where, :] = held
            sum_of = lambda value: jnp.sum(value, axis=0, keepdims=True)
            for sub, place in enumerate(places):
                owner, index = spots[sub]
                total0, total1, total2 = totals[sub]
                off_x = offsets[sub][0]
                wide = total0 * off_x
                moments = jnp.concatenate(
                    [
                        sum_of(total0),
                        sum_of(wide),
                        sum_of(total1),
                        sum_of(wide * off_x),
                        sum_of(total1 * off_x),
                        sum_of(total2),
                        jnp.zeros((2, splats), F32),
                    ],
                    axis=0,
                )
                tinted = dot32(cot_rows[...], pairs[place])
                grads[owner, index, 0:8, :] += moments
                grads[owner, index, 8:16, :] += (
                    tinted[:8, :splats] + tinted[8:, :splats] + tinted[:8, splats:]
                )
            return 0

        lax.fori_loop(0, steps, backward, 0)
        return 0

    lax.fori_loop(0, cameras * tiles, tile_step, 0)

    for index in range(cameras * cap):
        raw = [received_ref[:, index * PROJ + k, :] for k in range(PROJ)]
        turn_x, turn_y, conic_a, conic_c, turn_b, root = shape_of(raw)
        conic_b = 0.9 * root * turn_b
        sum0, sum_x, sum_y, sum_xx, sum_xy, sum_yy = [grads[:, index, k, :] for k in range(6)]
        grad_b = -sum_xy
        grad_a = -0.5 * sum_xx + grad_b * (0.5 * conic_b / conic_a)
        grad_c = -0.5 * sum_yy + grad_b * (0.5 * conic_b / conic_c)
        results = [
            (conic_a * sum_x + conic_b * sum_y) * (spread * (1.0 - turn_x * turn_x)),
            (conic_b * sum_x + conic_c * sum_y) * (spread * (1.0 - turn_y * turn_y)),
            grad_a * (0.1 * sigmoid(raw[2])),
            grad_b * (0.9 * root * (1.0 - turn_b * turn_b)),
            grad_c * (0.1 * sigmoid(raw[4])),
            sum0 * sigmoid(6.0 - raw[5]),
        ]
        for k in range(3):
            tone = sigmoid(raw[6 + k])
            results.append(grads[:, index, 8 + k, :] * (tone * (1.0 - tone)))
        for k in range(PROJ):
            back_ref[:, index * PROJ + k, :] = results[k]


def render(slots, counts, received, targets):
    owners, rows, splats = received.shape
    cameras, tiles, depth = slots.shape
    pixels = targets.shape[-1]
    cap = rows // (PROJ * cameras)
    depth = -(-depth // PAIR) * PAIR
    return pl.pallas_call(
        render_kernel,
        out_shape=(
            jax.ShapeDtypeStruct(targets.shape, F32),
            jax.ShapeDtypeStruct(received.shape, F32),
        ),
        in_specs=[SMEM, SMEM, VMEM, VMEM],
        out_specs=(VMEM, VMEM),
        scratch_shapes=[
            pltpu.VMEM((owners, cameras * cap, 16, splats), F32),
            pltpu.VMEM((owners, cameras * cap, 16, splats), F32),
            pltpu.VMEM((depth, pixels, splats), F32),
            pltpu.VMEM((depth, pixels, 2 * splats), BF16),
            pltpu.VMEM((depth, pixels, splats), F32),
            pltpu.VMEM((pixels, splats), F32),
            pltpu.VMEM((2 * splats, 2 * splats), BF16),
            pltpu.VMEM((2 * splats, 2 * splats), BF16),
            pltpu.VMEM((16, pixels), BF16),
            pltpu.VMEM((pixels, 128), BF16),
            pltpu.VMEM((8, pixels), F32),
        ],
        compiler_params=pltpu.CompilerParams(vmem_limit_bytes=BIG),
        cost_estimate=pl.CostEstimate(
            flops=20_000_000_000, bytes_accessed=100_000_000, transcendentals=4_000_000
        ),
        name="render",
    )(slots, counts, received, targets)


def update_kernel(groups, *refs):
    send_ref, split_ref, live_ref, back_ref, params_hbm = refs[:5]
    packs_hbm = refs[5 : 5 + groups]
    (params_out, first_out, second_out, parent_out) = refs[5 + groups : 9 + groups]
    table, slopes, params_ref, packs, arrivals = refs[9 + groups :]
    loads = [
        pltpu.make_async_copy(packs_hbm[turn], packs.at[turn], arrivals.at[turn])
        for turn in range(groups)
    ]
    loads.append(pltpu.make_async_copy(params_hbm, params_ref, arrivals.at[groups]))
    for load in loads:
        load.start()
    me = lax.axis_index("cam")
    owners, rows = back_ref.shape[1:3]
    values, share, splats = first_out.shape
    cameras = table.shape[1] // (16 * groups)
    cap = rows // (PROJ * cameras)
    table[...] = jnp.zeros(table.shape, F32)
    for turn in range(groups):
        for owner in range(owners):
            for camera in range(cameras):
                for place in range(cap):
                    block = send_ref[turn, (camera * cap + place) * owners + owner]
                    first = (camera * cap + place) * PROJ
                    into = (turn * cameras + camera) * 16
                    table[block, into : into + PROJ, :] += back_ref[
                        turn, owner, first : first + PROJ, :
                    ]
    held = values * share
    for load in loads:
        load.wait()
    stacked = jnp.concatenate(
        [packs[turn, 2 * held : 2 * held + 16 * cameras, :] for turn in range(groups)], axis=0
    )
    matrix_high, matrix_low = split2(stacked.T[: -(-values // 16) * 16])
    both = jnp.concatenate([matrix_high, matrix_low], axis=1)
    for turn in range(groups):
        base = pl.multiple_of(lax.rem(me + turn, groups) * share, share)
        for place in range(share):
            high, low = split2(table[base + place])
            gradient = dot32(both, jnp.concatenate([high, high], axis=0)) + dot32(matrix_high, low)
            slopes[:, place, :] = gradient[:values]
        pack = packs.at[turn]
        for start in range(0, values, 8):
            end = min(values, start + 8)
            size = (end - start, share, splats)
            gradient = slopes[start:end]
            first = pack[start * share : end * share, :].reshape(size)
            second = pack[held + start * share : held + end * share, :].reshape(size)
            new_first = BETA_FIRST * first + (1.0 - BETA_FIRST) * gradient
            new_second = BETA_SECOND * second + (1.0 - BETA_SECOND) * gradient * gradient
            params_out[start:end, pl.ds(base, share), :] = params_ref[
                start:end, pl.ds(base, share), :
            ] - RATE * new_first / (jnp.sqrt(new_second) + EPSILON)
            if turn == 0:
                first_out[start:end] = new_first
                second_out[start:end] = new_second
    for owner in range(split_ref.shape[1]):
        alive = live_ref[0, owner].astype(F32)
        chosen = params_out[:, pl.ds(split_ref[0, owner], 1), :].reshape(values, splats)
        parent_out[owner, 0:values, :] = chosen * alive
        parent_out[owner, values : values + 1, :] = jnp.zeros((1, splats), F32) + alive


def update(sends, split_block, split_live, back, params, packs, share, cameras):
    groups = len(packs)
    values, owned, splats = params.shape
    moments = jax.ShapeDtypeStruct((values, share, splats), F32)
    return pl.pallas_call(
        functools.partial(update_kernel, groups),
        out_shape=(
            jax.ShapeDtypeStruct(params.shape, F32),
            moments,
            moments,
            jax.ShapeDtypeStruct((split_block.shape[1], values + 1, splats), F32),
        ),
        in_specs=[SMEM, SMEM, SMEM, VMEM] + [pl.BlockSpec(memory_space=pl.ANY)] * (1 + groups),
        out_specs=(VMEM,) * 4,
        scratch_shapes=[
            pltpu.VMEM((owned, groups * 16 * cameras, splats), F32),
            pltpu.VMEM((values, share, splats), F32),
            pltpu.VMEM(params.shape, F32),
            pltpu.VMEM((groups,) + packs[0].shape, F32),
            pltpu.SemaphoreType.DMA((groups + 1,)),
        ],
        compiler_params=pltpu.CompilerParams(vmem_limit_bytes=BIG),
        name="update",
    )(sends, split_block, split_live, back, params, *packs)


def divide_kernel(parent_ref, child_ref):
    values = parent_ref.shape[1] - 1
    line = lax.broadcasted_iota(jnp.int32, (values, parent_ref.shape[2]), 0)
    for owner in range(parent_ref.shape[0]):
        alive = parent_ref[owner, values : values + 1, :]
        parent = parent_ref[owner, 0:values, :]
        shift = jnp.concatenate(
            [
                0.5 * jnp.exp(parent[3:6] - 1.0) * alive,
                jnp.zeros((values - 3, parent.shape[1]), F32),
            ],
            axis=0,
        )
        shrunk = parent - jnp.where((line >= 3) & (line < 6), SHRINK, 0.0) * alive
        child_ref[owner, :, 0, :] = shrunk + shift
        child_ref[owner, :, 1, :] = shrunk - shift


def divide(parents):
    owners, rows, splats = parents.shape
    return pl.pallas_call(
        divide_kernel,
        out_shape=jax.ShapeDtypeStruct((owners, rows - 1, 2, splats), F32),
        in_specs=[VMEM],
        out_specs=VMEM,
        compiler_params=pltpu.CompilerParams(vmem_limit_bytes=BIG),
        name="divide",
    )(parents)


def body(
    params, moment_first, moment_second, cam_proj, send_block,
    tile_slot, tile_count, targets, split_block, split_live,
):
    groups = lax.axis_size("cam")
    cameras, rows, values = cam_proj.shape
    owned, _, splats = params.shape
    share = moment_first.shape[2]
    matrix = jnp.pad(cam_proj, ((0, 0), (0, 16 - rows), (0, 128 - values)))
    matrix = matrix.reshape(cameras * 16, 128)
    send_block = send_block.transpose(0, 1, 3, 2)
    numbers = send_block.astype(F32).reshape(-1)
    numbers = jnp.pad(numbers, (0, -numbers.size % 1024)).reshape(-1, 128)
    by_value = lambda moment: moment[0, 0].transpose(1, 0, 2).reshape(values * share, splats)
    pack = jnp.concatenate([by_value(moment_first), by_value(moment_second), matrix, numbers])
    packs = [pack]
    for turn in range(1, groups):
        pattern = [((one + turn) % groups, one) for one in range(groups)]
        packs.append(lax.ppermute(pack, "cam", pattern))
    first_number = 2 * values * share + cameras * 16
    used = -(-send_block.size // 128)
    sends = jnp.stack([one[first_number : first_number + used].reshape(-1) for one in packs])
    sends = sends.astype(jnp.int32)

    by_block = params.transpose(1, 0, 2)
    received = project(send_block, matrix, by_block)
    images, back = render(tile_slot, tile_count, received, targets.transpose(0, 2, 1, 3))
    gathered = return_home(back, groups)
    new_params, new_first, new_second, parents = update(
        sends, split_block, split_live, gathered, by_block, packs, share, cameras
    )
    children = divide(exchange(parents, "dev", 6))
    restore = lambda moment: moment.transpose(1, 0, 2).reshape(moment_first.shape)
    return (
        images.transpose(0, 2, 1, 3),
        new_params.transpose(1, 0, 2),
        restore(new_first),
        restore(new_second),
        children.transpose(0, 2, 1, 3),
    )


def solution(mesh):
    placed = (
        P("dev", None, None),
        P("dev", "cam", None, None, None),
        P("dev", "cam", None, None, None),
        P("cam", None, None),
        P("cam", "dev", None, None),
        P("cam", "dev", None),
        P("cam", "dev"),
        P("cam", "dev", None, None),
        P("dev", None),
        P("dev", None),
    )
    return jax.shard_map(
        body,
        mesh=mesh,
        in_specs=placed,
        out_specs=(
            P("cam", "dev", None, None),
            P("dev", None, None),
            P("dev", "cam", None, None, None),
            P("dev", "cam", None, None, None),
            P("dev", None, None, None),
        ),
        check_vma=False,
    )
```

profile of v0, /device:TPU:1, one launch (start us, length us, event | category | flops | bytes accessed | tf_op | source)
XLA Modules:
  0.0 67.8 jit_solution(6217639838899184339)
XLA Ops:
  0.6 0.0 copy-start.5
  0.6 0.7 %bitcast_convert_fusion = f32[2,1,2,8]{3,2,1,0:T(2,128)S(1)} fusion(s32[2,1,8,2]{2,3,1,0:T(2,128)} %param.14), kind=kLoop, calls=%fused_computation.5 | loop fusion | flops 32 | bytes 256 | tf_op jit(solution)/shard_map/convert_element_type | solution.py:638
  1.3 0.1 reshape.33
  1.4 0.0 copy-done.5
  1.4 0.0 copy-start.4
  1.5 1.1 %pad_maximum_fusion.refs_5_ = f32[984,128]{1,0:T(8,128)S(1)} fusion(f32[8,128]{1,0:T(8,128)S(1)} %pad_bitcast_fusion, f32[32,128]{1,0:T(8,128)S(1)} %bitcast.33, f32[472,128]{1,0:T(8,128)} %bitcast.31, f32[472,128]{1,0:T(8,128)} %bitcast.32), kind=kLoop, calls=%fused_computation | loop fusion | flops 377856 | bytes 1007616 | tf_op jit(solution)/shard_map/concatenate | solution.py:641
  2.6 0.0 copy-done.4
  2.6 0.0 copy-start
  2.6 2.1 %collective-permute-start.2 = (f32[984,128]{1,0:T(8,128)S(1)}, f32[984,128]{1,0:T(8,128)S(1)}, u32[]{:S(2)}, u32[]{:S(2)}) collective-permute-start(f32[984,128]{1,0:T(8,128)S(1)} %pad_maximum_fusion.refs_5_), channel_id=1, source_target_pairs={{24,0},{0,8},{8,16},{16,24},{25,1},{1,9},{9,17},{17,25},{26,2},{2,... | collective-permute-start | bytes 1511432 | tf_op jit(solution)/shard_map/ppermute | solution.py:645
  4.7 1.2 %collective-permute-start.1 = (f32[984,128]{1,0:T(8,128)S(1)}, f32[984,128]{1,0:T(8,128)S(1)}, u32[]{:S(2)}, u32[]{:S(2)}) collective-permute-start(f32[984,128]{1,0:T(8,128)S(1)} %pad_maximum_fusion.refs_5_), channel_id=1, source_target_pairs={{16,0},{24,8},{0,16},{8,24},{17,1},{25,9},{1,17},{9,25},{18,2},{26... | collective-permute-start | bytes 1511432 | tf_op jit(solution)/shard_map/ppermute | solution.py:645
  5.9 1.2 %collective-permute-start = (f32[984,128]{1,0:T(8,128)S(1)}, f32[984,128]{1,0:T(8,128)S(1)}, u32[]{:S(2)}, u32[]{:S(2)}) collective-permute-start(f32[984,128]{1,0:T(8,128)S(1)} %pad_maximum_fusion.refs_5_), channel_id=1, source_target_pairs={{8,0},{16,8},{24,16},{0,24},{9,1},{17,9},{25,17},{1,25},{10,2},{18... | collective-permute-start | bytes 1511432 | tf_op jit(solution)/shard_map/ppermute | solution.py:645
  7.1 10.6 %project.1.received_ref = f32[8,36,128]{2,1,0:T(8,128)} custom-call(s32[2,1,2,8]{3,2,1,0:T(2,128)} %bitcast.35, f32[32,128]{1,0:T(8,128)} %bitcast.34, f32[59,32,128]{2,1,0:T(8,128)} %bitcast.28), custom_call_target="tpu_custom_call" | custom-call | tf_op jit(solution)/shard_map/project/pallas_call | solution.py:98
  17.7 0.0 copy-done
  17.7 15.6 %render.1 = (f32[2,3,2,256]{3,2,1,0:T(2,128)}, f32[8,36,128]{2,1,0:T(8,128)}) custom-call(s32[2,2,8]{2,1,0:T(2,128)} %slot_ref.1, s32[2,2]{1,0:T(2,128)} %count_ref.1, f32[8,36,128]{2,1,0:T(8,128)} %project.1.received_ref, f32[2,3,2,256]{3,2,1,0:T(2,128)} %bitcast.39), custom_call_target="tpu_custom_call" | custom-call | flops 20000000000 | bytes 100000000 | tf_op jit(solution)/shard_map/render/pallas_call | solution.py:478
  33.3 14.8 %return_home.1.refs_3_ = f32[4,8,36,128]{3,2,1,0:T(8,128)} custom-call(f32[8,36,128]{2,1,0:T(8,128)} %get-tuple-element.12.x_ref), custom_call_target="tpu_custom_call" | custom-call | tf_op jit(solution)/shard_map/return_home/pallas_call | solution.py:222
  48.1 0.0 collective-permute-done.2.refs_8_
  48.2 0.0 copy-start.1
  48.2 0.0 collective-permute-done.1.refs_7_
  48.2 0.0 copy-start.2
  48.2 0.0 collective-permute-done.refs_6_
  48.2 0.0 copy-start.3
  48.2 0.7 %maximum_convert_fusion.refs_0_ = s32[4,128]{1,0:T(4,128)} fusion(f32[1,128]{1,0:T(1,128)S(1)} %slice.22, f32[1,128]{1,0:T(1,128)S(1)} %slice.21, f32[1,128]{1,0:T(1,128)S(1)} %slice.20, f32[1,128]{1,0:T(1,128)S(1)} %fusion), kind=kLoop, calls=%fused_computation.3 | loop fusion | flops 2048 | bytes 4096 | tf_op jit(solution)/shard_map/convert_element_type | solution.py:649
  48.9 0.0 copy-done.1
  48.9 0.2 copy-done.2
  49.1 0.2 copy-done.3
  49.3 5.7 %update.1 = (f32[59,32,128]{2,1,0:T(8,128)}, f32[59,8,128]{2,1,0:T(8,128)}, f32[59,8,128]{2,1,0:T(8,128)}, f32[8,60,128]{2,1,0:T(8,128)}) custom-call(s32[4,128]{1,0:T(4,128)} %maximum_convert_fusion.refs_0_, s32[1,8]{1,0:T(1,128)} %refs_1_.1, s32[1,8]{1,0:T(1,128)} %refs_2_.1, f32[4,8,36,128]{3,2,1,0:T(8,128)} %return_home.1.refs_3_, ...), custom_call_target="tpu_custom_call" | custom-call | tf_op jit(solution)/shard_map/update/pallas_call | solution.py:575
  55.0 10.8 %exchange_6.1.parent_ref = f32[8,60,128]{2,1,0:T(8,128)} custom-call(f32[8,60,128]{2,1,0:T(8,128)} %get-tuple-element.16.x_ref), custom_call_target="tpu_custom_call" | custom-call | tf_op jit(solution)/shard_map/exchange_6/pallas_call | solution.py:149
  65.8 2.0 %divide.1 = f32[8,59,2,128]{3,2,1,0:T(2,128)} custom-call(f32[8,60,128]{2,1,0:T(8,128)} %exchange_6.1.parent_ref), custom_call_target="tpu_custom_call" | custom-call | tf_op jit(solution)/shard_map/divide/pallas_call | solution.py:617
  (7 shorter events, 0.0 us)
Async XLA Ops:
  0.6 0.8 %copy-start.5 = (f32[2,9,59]{2,0,1:T(2,128)S(1)}, f32[2,9,59]{2,0,1:T(2,128)}, u32[]{:S(2)}) copy-start(f32[2,9,59]{2,0,1:T(2,128)} %param.13) | copy-start | bytes 12748
  1.4 1.1 %copy-start.4 = (f32[2,16,128]{2,1,0:T(8,128)}, f32[2,16,128]{2,1,0:T(8,128)S(1)}, u32[]{:S(2)}) copy-start(f32[2,16,128]{2,1,0:T(8,128)S(1)} %pad.8.clone) | copy-start | bytes 49156
  2.6 15.1 %copy-start = (f32[984,128]{1,0:T(8,128)}, f32[984,128]{1,0:T(8,128)S(1)}, u32[]{:S(2)}) copy-start(f32[984,128]{1,0:T(8,128)S(1)} %pad_maximum_fusion.refs_5_) | copy-start | bytes 1511428
  2.6 45.6 %collective-permute-start.2 = (f32[984,128]{1,0:T(8,128)S(1)}, f32[984,128]{1,0:T(8,128)S(1)}, u32[]{:S(2)}, u32[]{:S(2)}) collective-permute-start(f32[984,128]{1,0:T(8,128)S(1)} %pad_maximum_fusion.refs_5_), channel_id=1, source_target_pairs={{24,0},{0,8},{8,16},{16,24},{25,1},{1,9},{9,17},{17,25},{26,2},{2,... | collective-permute-start | bytes 1511432 | tf_op jit(solution)/shard_map/ppermute | solution.py:645
  4.7 43.5 %collective-permute-start.1 = (f32[984,128]{1,0:T(8,128)S(1)}, f32[984,128]{1,0:T(8,128)S(1)}, u32[]{:S(2)}, u32[]{:S(2)}) collective-permute-start(f32[984,128]{1,0:T(8,128)S(1)} %pad_maximum_fusion.refs_5_), channel_id=1, source_target_pairs={{16,0},{24,8},{0,16},{8,24},{17,1},{25,9},{1,17},{9,25},{18,2},{26... | collective-permute-start | bytes 1511432 | tf_op jit(solution)/shard_map/ppermute | solution.py:645
  5.9 42.3 %collective-permute-start = (f32[984,128]{1,0:T(8,128)S(1)}, f32[984,128]{1,0:T(8,128)S(1)}, u32[]{:S(2)}, u32[]{:S(2)}) collective-permute-start(f32[984,128]{1,0:T(8,128)S(1)} %pad_maximum_fusion.refs_5_), channel_id=1, source_target_pairs={{8,0},{16,8},{24,16},{0,24},{9,1},{17,9},{25,17},{1,25},{10,2},{18... | collective-permute-start | bytes 1511432 | tf_op jit(solution)/shard_map/ppermute | solution.py:645
  48.2 0.8 %copy-start.1 = (f32[984,128]{1,0:T(8,128)}, f32[984,128]{1,0:T(8,128)S(1)}, u32[]{:S(2)}) copy-start(f32[984,128]{1,0:T(8,128)S(1)} %collective-permute-done.2.refs_8_) | copy-start | bytes 1511428
  48.2 0.9 %copy-start.2 = (f32[984,128]{1,0:T(8,128)}, f32[984,128]{1,0:T(8,128)S(1)}, u32[]{:S(2)}) copy-start(f32[984,128]{1,0:T(8,128)S(1)} %collective-permute-done.1.refs_7_) | copy-start | bytes 1511428
  48.2 1.1 %copy-start.3 = (f32[984,128]{1,0:T(8,128)}, f32[984,128]{1,0:T(8,128)S(1)}, u32[]{:S(2)}) copy-start(f32[984,128]{1,0:T(8,128)S(1)} %collective-permute-done.refs_6_) | copy-start | bytes 1511428
where the time goes:
time: 67.7 us; the launch traced here: 67.8 us
  Pallas kernels  59.6 us (88%)
  starting transfers between devices  4.47 us (7%)
  other arithmetic  2.47 us (4%)
  between operations  0.8 us (1%)
    pallas_call x1, Pallas kernels, render(): pl.pallas_call(render_kernel, out_shape=(jax.ShapeDtypeStruct(targets.sha...  15.6 us
    pallas_call x1, Pallas kernels, return_home(): pl.pallas_call(functools.partial(return_kernel, owners, groups), out_shap...  14.8 us
    pallas_call x1, Pallas kernels, exchange(): pl.pallas_call(functools.partial(exchange_kernel, axis, count), out_shape...  10.8 us
    pallas_call x1, Pallas kernels, project(): pl.pallas_call(project_kernel, out_shape=jax.ShapeDtypeStruct(shape, F32)...  10.6 us
    pallas_call x1, Pallas kernels, update(): pl.pallas_call(functools.partial(update_kernel, groups), out_shape=(jax.S...  5.71 us
    ppermute x3, starting transfers between devices, body(): packs.append(lax.ppermute(pack, 'cam', pattern))  4.47 us
    pallas_call x1, Pallas kernels, divide(): pl.pallas_call(divide_kernel, out_shape=jax.ShapeDtypeStruct((owners, row...  2 us
  transfers between devices with their start and end apart: 3, of which 0 were waited for; matrix products, arithmetic and copies ran while one was open for 0% of the time, Pallas kernels for 61%

commit v1 on v0

v1 whole, which is shorter than its diff:
```python
import functools
import math

import jax
import jax.numpy as jnp
from jax import lax
from jax.experimental import pallas as pl
from jax.experimental.pallas import tpu as pltpu
from jax.sharding import PartitionSpec as P

TSIDE = 16
PROJ = 9
PAIR = 2
LOSS_WEIGHT = 256.0
RATE = 0.01
BETA_FIRST = 0.9
BETA_SECOND = 0.999
EPSILON = 1e-08
SHRINK = math.log(1.6)
LOG2E = math.log2(math.e)
MESH = pl.DeviceIdType.MESH
F32 = jnp.float32
BF16 = jnp.bfloat16
VMEM = pl.BlockSpec(memory_space=pltpu.VMEM)
SMEM = pl.BlockSpec(memory_space=pltpu.SMEM)
ANY = pl.BlockSpec(memory_space=pl.ANY)
BIG = 60 * 1024 * 1024
HALF = 128
SAVED = 14


def padded(size, unit):
    return -(-size // unit) * unit


def split2(value):
    high = value.astype(BF16)
    return high, (value - high.astype(F32)).astype(BF16)


def dot32(left, right, dims=(((1,), (0,)), ((), ()))):
    return lax.dot_general(left, right, dims, preferred_element_type=F32)


def softplus(value):
    return jnp.maximum(value, 0.0) + jnp.log(1.0 + jnp.exp(-jnp.abs(value)))


def sigmoid(value):
    return 1.0 / (1.0 + jnp.exp(-value))


def left3(value, width):
    high, low = split2(value)
    high = high.astype(F32)[:, :width]
    low = low.astype(F32)[:, :width]
    return jnp.concatenate([high, low, high], axis=1).astype(BF16)


def right3(value):
    high, low = split2(value)
    return jnp.concatenate([high, high, low], axis=0)


def send(src, dst, send_sem, recv_sem, axis, peer):
    copy = pltpu.make_async_remote_copy(
        src_ref=src,
        dst_ref=dst,
        send_sem=send_sem,
        recv_sem=recv_sem,
        device_id={axis: peer},
        device_id_type=MESH,
    )
    copy.start()
    return copy


def keep(src, dst, sem):
    copy = pltpu.make_async_copy(src, dst, sem)
    copy.start()
    return copy


def make_features(raw_ref, camera, place, cap, feats, saved):
    index = camera * cap + place
    raw = [raw_ref[index, k] for k in range(PROJ)]
    centre = 0.5 * TSIDE
    spread = 0.375 * TSIDE
    turn_x = jnp.tanh(raw[0])
    turn_y = jnp.tanh(raw[1])
    conic_a = 0.02 + 0.1 * softplus(raw[2])
    conic_c = 0.02 + 0.1 * softplus(raw[4])
    turn_b = jnp.tanh(raw[3])
    root = jnp.sqrt(conic_a * conic_c)
    conic_b = 0.9 * root * turn_b
    owners, splats = raw[0].shape
    flat = feats.reshape(feats.shape[0] * 16, splats)

    def put(k, value):
        first = (camera * cap * owners + place) * 16 + k
        flat[pl.ds(first, owners, stride=cap * 16), :] = value

    put(0, centre + spread * turn_x)
    put(1, centre + spread * turn_y)
    put(2, (0.5 * LOG2E) * conic_a)
    put(3, LOG2E * conic_b)
    put(4, (0.5 * LOG2E) * conic_c)
    put(5, math.log2(0.99) - LOG2E * softplus(6.0 - raw[5]))
    saved[index, 0] = conic_a
    saved[index, 1] = conic_b
    saved[index, 2] = conic_c
    saved[index, 3] = spread * (1.0 - turn_x * turn_x)
    saved[index, 4] = spread * (1.0 - turn_y * turn_y)
    saved[index, 5] = 0.1 * sigmoid(raw[2])
    saved[index, 6] = 0.9 * root * (1.0 - turn_b * turn_b)
    saved[index, 7] = 0.1 * sigmoid(raw[4])
    saved[index, 8] = sigmoid(6.0 - raw[5])
    saved[index, 9] = 0.5 * conic_b / conic_a
    saved[index, 10] = 0.5 * conic_b / conic_c
    for k in range(3):
        tone = sigmoid(raw[6 + k])
        put(8 + k, tone)
        saved[index, 11 + k] = tone * (1.0 - tone)


def return_planes(sums, saved, index, back):
    sum0, sum_x, sum_y, sum_xx, sum_xy, sum_yy = sums[:6]
    part = lambda k: saved[index, k]
    grad_b = -sum_xy
    back[index, 0] = (part(0) * sum_x + part(1) * sum_y) * part(3)
    back[index, 1] = (part(1) * sum_x + part(2) * sum_y) * part(4)
    back[index, 2] = (grad_b * part(9) - 0.5 * sum_xx) * part(5)
    back[index, 3] = grad_b * part(6)
    back[index, 4] = (grad_b * part(10) - 0.5 * sum_yy) * part(7)
    back[index, 5] = sum0 * part(8)
    for k in range(3):
        back[index, 6 + k] = sums[6 + k] * part(11 + k)


def render_tile(
    camera, tile, slot_ref, count_ref, target_ref, image_ref,
    feats, entries, weights, pairs, ratios, carry, before, after_tri, cot_rows, cot_cols,
    picture,
):
    depth = slot_ref.shape[2]
    splats = feats.shape[2]
    slots = feats.shape[0] // slot_ref.shape[0]
    pixels = TSIDE * TSIDE
    chunks = pixels // HALF
    per_chunk = HALF // TSIDE
    steps = depth // PAIR
    grid = lax.broadcasted_iota(jnp.int32, (TSIDE, splats), 0).astype(F32) + 0.5
    pad_rows = jnp.zeros((8, splats), F32)
    live = count_ref[camera, tile]
    carry[...] = jnp.zeros(carry.shape, F32)
    picture[...] = jnp.zeros(picture.shape, F32)

    def entry_of(place):
        slot = jnp.clip(slot_ref[camera, tile, place], 0, slots - 1)
        return feats[camera * slots + slot]

    def forward(pair, _):
        places = [PAIR * pair + sub for sub in range(PAIR)]
        alphas, logs, sums, shades = [], [], [], []
        for place in places:
            entry = entry_of(place)
            part = lambda k: entry[k : k + 1]
            off_x = grid - part(0)
            off_y = grid - part(1)
            in_x = -(part(2) * off_x * off_x)
            cross = -(part(3) * off_x)
            faint = part(5) + jnp.where(place < live, 0.0, -1e30)
            in_y = faint - part(4) * off_y * off_y
            for chunk in range(chunks):
                lines = []
                for line in range(chunk * per_chunk, (chunk + 1) * per_chunk):
                    lines.append(in_x + (in_y[line : line + 1] + cross * off_y[line : line + 1]))
                alpha = jnp.exp2(jnp.concatenate(lines, axis=0))
                log_keep = jnp.log2(1.0 - alpha)
                alphas.append(alpha)
                logs.append(log_keep)
                sums.append(dot32(jnp.concatenate(split2(log_keep), axis=1), before[...]))
            colour_high, colour_low = split2(entry[8:16])
            colour_high = colour_high.astype(F32)
            colour_low = colour_low.astype(F32)
            shades.append(
                jnp.concatenate(
                    [
                        jnp.concatenate([colour_high, colour_low], axis=0),
                        jnp.concatenate([colour_high, pad_rows], axis=0),
                    ],
                    axis=1,
                ).astype(BF16)
            )
        for chunk in range(chunks):
            where = slice(chunk * HALF, (chunk + 1) * HALF)
            held = carry[where, :]
            drawn = jnp.zeros((16, HALF), F32)
            for sub, place in enumerate(places):
                at = sub * chunks + chunk
                weight = alphas[at] * jnp.exp2(sums[at][:, :splats] + held)
                held = held + sums[at][:, splats:]
                both = jnp.concatenate(split2(weight), axis=1)
                weights[place, where, :] = weight
                pairs[place, where, :] = both
                ratios[place, where, :] = alphas[at] * jnp.exp2(-logs[at])
                drawn += dot32(shades[sub], both, (((1,), (1,)), ((), ())))
            carry[where, :] = held
            picture[:, where] += drawn[:8] + drawn[8:]
        return 0

    lax.fori_loop(0, steps, forward, 0)
    for k in range(3):
        colour = picture[k : k + 1, :]
        image_ref[camera, k, pl.ds(tile, 1), :] = colour
        picture[k : k + 1, :] = LOSS_WEIGHT * (colour - target_ref[camera, k, pl.ds(tile, 1), :])
    cot_high, cot_low = split2(picture[...])
    cot_high = cot_high.astype(F32)
    cot_low = cot_low.astype(F32)
    cot_rows[...] = jnp.concatenate([cot_high, cot_low], axis=0).astype(BF16)
    stacked = jnp.concatenate(
        [cot_high, cot_low, cot_high, jnp.zeros((HALF - 24, pixels), F32)], axis=0
    )
    cot_cols[...] = stacked.T.astype(BF16)
    carry[...] = jnp.zeros(carry.shape, F32)

    def backward(reverse, _):
        places = [PAIR * (steps - 1 - reverse) + PAIR - 1 - sub for sub in range(PAIR)]
        offsets, shaded, sums = [], [], []
        for place in places:
            entry = entry_of(place)
            part = lambda k: entry[k : k + 1]
            offsets.append((grid - part(0), grid - part(1)))
            colour_high, colour_low = split2(entry[8:16])
            colour_high = colour_high.astype(F32)
            shades = jnp.concatenate(
                [
                    colour_high,
                    colour_high,
                    colour_low.astype(F32),
                    jnp.zeros((HALF - 24, splats), F32),
                ],
                axis=0,
            ).astype(BF16)
            for chunk in range(chunks):
                where = slice(chunk * HALF, (chunk + 1) * HALF)
                piece = dot32(cot_cols[where, :], shades) * weights[place, where, :]
                shaded.append(piece)
                sums.append(dot32(jnp.concatenate(split2(piece), axis=1), after_tri[...]))
        totals = [[jnp.zeros((TSIDE, splats), F32)] * 3 for _ in places]
        for chunk in range(chunks):
            where = slice(chunk * HALF, (chunk + 1) * HALF)
            held = carry[where, :]
            for sub, place in enumerate(places):
                at = sub * chunks + chunk
                pull = shaded[at] - (sums[at][:, :splats] + held) * ratios[place, where, :]
                held = held + sums[at][:, splats:]
                total0, total1, total2 = totals[sub]
                off_y = offsets[sub][1]
                for line in range(per_chunk):
                    height = off_y[chunk * per_chunk + line : chunk * per_chunk + line + 1]
                    piece = pull[line * TSIDE : (line + 1) * TSIDE]
                    lifted = piece * height
                    total0 += piece
                    total1 += lifted
                    total2 += lifted * height
                totals[sub] = [total0, total1, total2]
            carry[where, :] = held
        sum_of = lambda value: jnp.sum(value, axis=0, keepdims=True)
        for sub, place in enumerate(places):
            total0, total1, total2 = totals[sub]
            off_x = offsets[sub][0]
            wide = total0 * off_x
            tinted = dot32(cot_rows[...], pairs[place])
            tinted = tinted[:8, :splats] + tinted[8:, :splats] + tinted[:8, splats:]
            rows = [
                sum_of(total0),
                sum_of(wide),
                sum_of(total1),
                sum_of(wide * off_x),
                sum_of(total1 * off_x),
                sum_of(total2),
            ] + [tinted[k : k + 1] for k in range(3)]
            at = tile * depth + place
            for k in range(PROJ):
                entries[k, pl.ds(at, 1), :] = rows[k]
        return 0

    lax.fori_loop(0, steps, backward, 0)


def adam(gradient, value, first, second):
    new_first = BETA_FIRST * first + (1.0 - BETA_FIRST) * gradient
    new_second = BETA_SECOND * second + (1.0 - BETA_SECOND) * gradient * gradient
    return value - RATE * new_first / (jnp.sqrt(new_second) + EPSILON), new_first, new_second


def step_kernel(
    send_ref, slot_ref, count_ref, split_ref, live_ref, target_ref, proj_ref,
    params_hbm, first_hbm, second_hbm,
    image_ref, params_out, moments_out, child_out,
    meta, blocks, moments, parcels, raw, feats, saved, entries, back, gathered, table,
    fresh, new_moments, parents, landed, children,
    weights, pairs, ratios, carry, before, after_tri, cot_rows, cot_cols, picture,
    load_sems, meta_sems, moment_sems, raw_sems, back_sems, cross_sems, parent_sems, out_sems,
    child_sems, own_sems,
):
    cameras, _, cap, owners = send_ref.shape
    _, tiles, depth = slot_ref.shape
    values, owned, splats = params_hbm.shape
    share = first_hbm.shape[1]
    groups = meta.shape[0]
    me = lax.axis_index("dev")
    group = lax.axis_index("cam")
    slots = cap * owners
    lists = tiles * depth
    pad = padded(values, 16)
    rows = groups * cameras * PROJ
    high_rows = table.shape[1]
    flat_table = table.reshape(owned * high_rows, splats)
    peer_dev = [lax.rem(me + step, owners) for step in range(owners)]
    from_dev = [lax.rem(me - step + owners, owners) for step in range(owners)]
    peer_cam = [lax.rem(group + turn, groups) for turn in range(groups)]
    from_cam = [lax.rem(group - turn + groups, groups) for turn in range(groups)]

    barrier = pltpu.get_barrier_semaphore()
    for step in range(1, owners):
        pl.semaphore_signal(barrier, inc=1, device_id={"dev": peer_dev[step]}, device_id_type=MESH)
    for turn in range(1, groups):
        pl.semaphore_signal(barrier, inc=1, device_id={"cam": peer_cam[turn]}, device_id_type=MESH)

    for block in range(owned):
        blocks[block, values:pad, :] = jnp.zeros((pad - values, splats), F32)
    loads = [
        keep(params_hbm.at[:, block, :], blocks.at[block, pl.ds(0, values), :], load_sems.at[block])
        for block in range(owned)
    ]

    lane = lax.broadcasted_iota(jnp.int32, (8, 128), 1)
    sub = lax.broadcasted_iota(jnp.int32, (8, 128), 0)
    meta[group] = jnp.zeros(meta.shape[1:], F32)
    numbers = jnp.zeros((8, 128), F32)
    for camera in range(cameras):
        for place in range(cap):
            for owner in range(owners):
                number = send_ref[camera, 0, place, owner].astype(F32)
                numbers = jnp.where(
                    (lane == place * owners + owner) & (sub == camera), number, numbers
                )
        for k in range(PROJ):
            meta[group, camera * PROJ + k : camera * PROJ + k + 1, 0:values] = proj_ref[
                k, camera : camera + 1, :
            ]
    meta_rows = meta.shape[1]
    meta[group, meta_rows - 8 : meta_rows, :] = numbers

    matrices = []
    for camera in range(cameras):
        own = meta[group, camera * PROJ : (camera + 1) * PROJ, :]
        own = jnp.concatenate([own, jnp.zeros((16 - PROJ, 128), F32)], axis=0)
        matrices.append(left3(own, pad))

    row = lax.broadcasted_iota(jnp.int32, (splats, splats), 0)
    column = lax.broadcasted_iota(jnp.int32, (splats, splats), 1)
    ones = jnp.ones((splats, splats), BF16)
    lower = jnp.where(row < column, 1.0, 0.0).astype(BF16)
    upper = jnp.where(row > column, 1.0, 0.0).astype(BF16)
    for part in range(2):
        before[part * splats : (part + 1) * splats, :splats] = lower
        before[part * splats : (part + 1) * splats, splats:] = ones
        after_tri[part * splats : (part + 1) * splats, :splats] = upper
        after_tri[part * splats : (part + 1) * splats, splats:] = ones
    feats[...] = jnp.zeros(feats.shape, F32)

    for load in loads:
        load.wait()
    for camera in range(cameras):
        items = [(place, owner) for owner in range(owners) for place in range(cap)]
        for start in range(0, len(items), 2):
            couple = items[start : start + 2]
            right = jnp.concatenate(
                [right3(blocks[send_ref[camera, 0, place, owner]]) for place, owner in couple],
                axis=1,
            )
            result = dot32(matrices[camera], right)
            for number, (place, owner) in enumerate(couple):
                parcels[owner, camera * cap + place] = result[
                    :, number * splats : (number + 1) * splats
                ]

    pl.semaphore_wait(barrier, owners + groups - 2)
    raw_copies = []
    for step in range(1, owners):
        raw_copies.append(
            send(
                parcels.at[peer_dev[step], :, pl.ds(0, PROJ), :], raw.at[:, :, me, :],
                raw_sems.at[0, step - 1], raw_sems.at[1, step - 1], "dev", peer_dev[step],
            )
        )
    own_raw = keep(parcels.at[me, :, pl.ds(0, PROJ), :], raw.at[:, :, me, :], own_sems.at[0])
    meta_copies, moment_copies = [], []
    for turn in range(1, groups):
        meta_copies.append(
            send(
                meta.at[group], meta.at[group],
                meta_sems.at[0, turn - 1], meta_sems.at[1, turn - 1], "cam", peer_cam[turn],
            )
        )
    for turn in range(1, groups):
        for kind, source in enumerate((first_hbm, second_hbm)):
            for place in range(share):
                moment_copies.append(
                    send(
                        source.at[:, place, :],
                        moments.at[kind, group * share + place, pl.ds(0, values), :],
                        moment_sems.at[0, turn - 1, kind, place],
                        moment_sems.at[1, turn - 1, kind, place],
                        "cam", peer_cam[turn],
                    )
                )
    own_moments = [
        keep(
            source.at[:, place, :],
            moments.at[kind, group * share + place, pl.ds(0, values), :],
            moment_sems.at[0, groups - 1, kind, place],
        )
        for kind, source in enumerate((first_hbm, second_hbm))
        for place in range(share)
    ]

    one_hots = []
    entry_lane = lax.broadcasted_iota(jnp.int32, (slots, lists), 1)
    slot_row = lax.broadcasted_iota(jnp.int32, (slots, lists), 0)
    slot_row = lax.rem(slot_row, owners) * cap + lax.div(slot_row, owners)
    for camera in range(cameras):
        ids = jnp.full((slots, lists), -1, jnp.int32)
        for tile in range(tiles):
            for place in range(depth):
                slot = slot_ref[camera, tile, place]
                slot = jnp.where(place < count_ref[camera, tile], slot, -1)
                ids = jnp.where(entry_lane == tile * depth + place, slot, ids)
        hot = jnp.where(ids == slot_row, 1.0, 0.0)
        one_hots.append(jnp.concatenate([hot, hot], axis=1).astype(BF16))

    own_raw.wait()
    for copy in raw_copies:
        copy.wait_recv()
    for camera in range(cameras):
        for place in range(cap):
            make_features(raw, camera, place, cap, feats, saved)

    def render(camera, tile):
        render_tile(
            camera, tile, slot_ref, count_ref, target_ref, image_ref, feats, entries,
            weights, pairs, ratios, carry, before, after_tri, cot_rows, cot_cols, picture,
        )

    def slot_sums(camera):
        planes = []
        for start in range(0, PROJ, 2):
            kinds = list(range(start, min(start + 2, PROJ)))
            right = jnp.concatenate(
                [jnp.concatenate(split2(entries[k]), axis=0) for k in kinds], axis=1
            )
            result = dot32(one_hots[camera], right)
            for number in range(len(kinds)):
                planes.append(result[:, number * splats : (number + 1) * splats])
        for place in range(cap):
            part = [plane[place * owners : (place + 1) * owners] for plane in planes]
            return_planes(part, saved, camera * cap + place, back)

    back_copies = [[] for _ in range(cameras)]
    cross_copies = [[] for _ in range(cameras)]
    own_back = []

    def send_back(camera):
        mine = pl.ds(camera * cap, cap)
        for step in range(1, owners):
            back_copies[camera].append(
                send(
                    back.at[mine, :, peer_dev[step], :], gathered.at[group, mine, :, me, :],
                    back_sems.at[0, camera, step - 1], back_sems.at[1, camera, step - 1],
                    "dev", peer_dev[step],
                )
            )
        own_back.append(
            keep(
                back.at[mine, :, me, :], gathered.at[group, mine, :, me, :], own_sems.at[1 + camera]
            )
        )

    def send_across(camera):
        mine = pl.ds(camera * cap, cap)
        for step in range(owners):
            source = from_dev[step]
            if step:
                back_copies[camera][step - 1].wait_recv()
            else:
                own_back[camera].wait()
            piece = gathered.at[group, mine, :, source, :]
            for turn in range(1, groups):
                cross_copies[camera].append(
                    send(
                        piece, piece,
                        cross_sems.at[0, camera, turn - 1, step],
                        cross_sems.at[1, camera, turn - 1, step],
                        "cam", peer_cam[turn],
                    )
                )

    def scatter(turn, camera):
        origin = from_cam[turn]
        base = meta.shape[1] - 8
        ids = meta[origin, base + camera : base + camera + 1, :][:, :slots]
        block_row = lax.broadcasted_iota(jnp.int32, (owned, slots), 0).astype(F32)
        hot = jnp.where(jnp.broadcast_to(ids, (owned, slots)) == block_row, 1.0, 0.0)
        left = jnp.concatenate([hot, hot], axis=1).astype(BF16)
        for start in range(0, PROJ, 2):
            kinds = list(range(start, min(start + 2, PROJ)))
            sides = []
            for k in kinds:
                plane = jnp.concatenate(
                    [gathered[origin, camera * cap + place, k] for place in range(cap)], axis=0
                )
                sides.append(jnp.concatenate(split2(plane), axis=0))
            result = dot32(left, jnp.concatenate(sides, axis=1))
            for number, k in enumerate(kinds):
                flat_table[pl.ds((turn * cameras + camera) * PROJ + k, owned, stride=high_rows), :] = (
                    result[:, number * splats : (number + 1) * splats]
                )

    for camera in range(cameras):
        for tile in range(tiles):
            render(camera, tile)
            if camera and tile == 0:
                send_across(camera - 1)
        slot_sums(camera)
        send_back(camera)
    table[:, rows:high_rows, :] = jnp.zeros((owned, high_rows - rows, splats), F32)
    for copy in meta_copies:
        copy.wait_recv()
    stack = []
    for turn in range(groups):
        stack.append(meta[from_cam[turn], 0 : cameras * PROJ, :])
    stack.append(jnp.zeros((128 * -(-rows // 128) - rows, 128), F32))
    turned = jnp.concatenate(stack, axis=0).T
    left = left3(turned[:pad], high_rows)
    send_across(cameras - 1)
    for camera in range(cameras):
        scatter(0, camera)
    for camera in range(cameras):
        for turn in range(1, groups):
            for step in range(owners):
                cross_copies[camera][step * (groups - 1) + turn - 1].wait_recv()
            scatter(turn, camera)
    for copy in moment_copies:
        copy.wait_recv()
    for copy in own_moments:
        copy.wait()

    def gradients(couple):
        right = jnp.concatenate([right3(table[block]) for block in couple], axis=1)
        result = dot32(left, right)
        return [result[:, at * splats : (at + 1) * splats] for at in range(len(couple))]

    line = lax.broadcasted_iota(jnp.int32, (pad, splats), 0)
    for start in range(0, owners, 2):
        couple = list(range(start, min(start + 2, owners)))
        chosen = [split_ref[0, owner] for owner in couple]
        for owner, block, gradient in zip(couple, chosen, gradients(chosen)):
            alive = live_ref[0, owner].astype(F32)
            new_value, _, _ = adam(gradient, blocks[block], moments[0, block], moments[1, block])
            new_value = jnp.where(line < values, new_value, 1.0)
            parents[owner] = new_value * alive
    parent_copies = []
    for step in range(1, owners):
        parent_copies.append(
            send(
                parents.at[peer_dev[step], pl.ds(0, values + 1), :],
                landed.at[me, pl.ds(0, values + 1), :],
                parent_sems.at[0, step - 1], parent_sems.at[1, step - 1], "dev", peer_dev[step],
            )
        )
    own_parent = keep(
        parents.at[me, pl.ds(0, values + 1), :], landed.at[me, pl.ds(0, values + 1), :],
        own_sems.at[1 + cameras],
    )
    outs = []
    for start in range(0, owned, 2):
        couple = list(range(start, min(start + 2, owned)))
        for block, gradient in zip(couple, gradients(couple)):
            new_value, new_first, new_second = adam(
                gradient, blocks[block], moments[0, block], moments[1, block]
            )
            fresh[block] = new_value
            new_moments[0, block] = new_first
            new_moments[1, block] = new_second
            outs.append(
                keep(fresh.at[block], params_out.at[block], out_sems.at[block])
            )
    outs.append(
        keep(
            new_moments.at[:, pl.ds(group * share, share)], moments_out, own_sems.at[2 + cameras]
        )
    )
    for step in range(owners):
        source = from_dev[step]
        if step:
            parent_copies[step - 1].wait_recv()
        else:
            own_parent.wait()
        parent = landed[source]
        alive = parent[values : values + 1]
        shift = jnp.concatenate(
            [0.5 * jnp.exp(parent[0:8] - 1.0) * alive], axis=0
        )
        shift = jnp.concatenate([shift[3:6], jnp.zeros((pad - 3, splats), F32)], axis=0)
        shrunk = parent - jnp.where((line >= 3) & (line < 6), SHRINK, 0.0) * alive
        children[source, 0] = shrunk + shift
        children[source, 1] = shrunk - shift
        outs.append(keep(children.at[source], child_out.at[source], child_sems.at[step]))
    for copy in outs:
        copy.wait()
    for copy in raw_copies + meta_copies + moment_copies + parent_copies:
        copy.wait_send()
    for camera in range(cameras):
        for copy in back_copies[camera] + cross_copies[camera]:
            copy.wait_send()


def spread_kernel(
    image_ref, fresh_ref, moments_ref, children_ref,
    image_out, params_out, first_out, second_out, child_out,
    fresh, moments, children, in_sems, out_sems,
):
    owned = fresh.shape[0]
    owners = children.shape[0]
    share = moments.shape[1]
    values = params_out.shape[0]
    lump = 8
    loads, jobs = [], []
    for start in range(0, owned, lump):
        some = pl.ds(start, min(lump, owned - start))
        loads.append((fresh_ref.at[some], fresh.at[some]))
        jobs.append(
            [
                (fresh.at[block, pl.ds(0, values), :], params_out.at[:, block, :])
                for block in range(start, min(start + lump, owned))
            ]
        )
    for start in range(0, owners, lump):
        some = pl.ds(start, min(lump, owners - start))
        loads.append((children_ref.at[some], children.at[some]))
        jobs.append(
            [
                (children.at[source, kind, pl.ds(0, values), :], child_out.at[source, :, kind, :])
                for source in range(start, min(start + lump, owners))
                for kind in range(2)
            ]
        )
    for kind, target in enumerate((first_out, second_out)):
        loads.append((moments_ref.at[kind], moments.at[kind]))
        jobs.append(
            [
                (moments.at[kind, place, pl.ds(0, values), :], target.at[:, place, :])
                for place in range(share)
            ]
        )
    started = [keep(src, dst, in_sems.at[number]) for number, (src, dst) in enumerate(loads)]
    image_out[...] = image_ref[...]
    outs = []
    for copy, job in zip(started, jobs):
        copy.wait()
        for src, dst in job:
            outs.append(keep(src, dst, out_sems.at[len(outs)]))
    for copy in outs:
        copy.wait()


def spread_out(images, fresh, new_moments, children, values):
    owned, pad, splats = fresh.shape
    share = new_moments.shape[1]
    owners = children.shape[0]
    shape = jax.ShapeDtypeStruct
    return pl.pallas_call(
        spread_kernel,
        out_shape=(
            shape(images.shape, F32),
            shape((values, owned, splats), F32),
            shape((values, share, splats), F32),
            shape((values, share, splats), F32),
            shape((owners, values, 2, splats), F32),
        ),
        in_specs=[VMEM, ANY, ANY, ANY],
        out_specs=(VMEM, ANY, ANY, ANY, ANY),
        scratch_shapes=[
            pltpu.VMEM(fresh.shape, F32),
            pltpu.VMEM(new_moments.shape, F32),
            pltpu.VMEM(children.shape, F32),
            pltpu.SemaphoreType.DMA((owned + owners + 2,)),
            pltpu.SemaphoreType.DMA((owned + 2 * owners + 2 * share,)),
        ],
        compiler_params=pltpu.CompilerParams(vmem_limit_bytes=BIG),
        name="spread",
    )(images, fresh, new_moments, children)


def body(
    params, moment_first, moment_second, cam_proj, send_block,
    tile_slot, tile_count, targets, split_block, split_live,
):
    groups = lax.axis_size("cam")
    cameras, _, values = cam_proj.shape
    owned, _, splats = params.shape
    share = moment_first.shape[2]
    owners, cap = send_block.shape[2:]
    _, tiles, depth = tile_slot.shape
    pixels = targets.shape[-1]
    depth = padded(depth, PAIR)
    pad = padded(values, 16)
    indices = cameras * cap
    rows = groups * cameras * PROJ
    high_rows = padded(rows, 16)
    meta_rows = padded(cameras * PROJ, 8) + 8
    by_value = lambda moment: moment[0, 0].transpose(1, 0, 2)
    shape = jax.ShapeDtypeStruct
    dma = pltpu.SemaphoreType.DMA
    scratch = [
        pltpu.VMEM((groups, meta_rows, 128), F32),
        pltpu.VMEM((owned, pad, splats), F32),
        pltpu.VMEM((2, owned, pad, splats), F32),
        pltpu.VMEM((owners, indices, 16, splats), F32),
        pltpu.VMEM((indices, PROJ, owners, splats), F32),
        pltpu.VMEM((indices * owners, 16, splats), F32),
        pltpu.VMEM((indices, SAVED, owners, splats), F32),
        pltpu.VMEM((PROJ, tiles * depth, splats), F32),
        pltpu.VMEM((indices, PROJ, owners, splats), F32),
        pltpu.VMEM((groups, indices, PROJ, owners, splats), F32),
        pltpu.VMEM((owned, high_rows, splats), F32),
        pltpu.VMEM((owned, pad, splats), F32),
        pltpu.VMEM((2, owned, pad, splats), F32),
        pltpu.VMEM((owners, pad, splats), F32),
        pltpu.VMEM((owners, pad, splats), F32),
        pltpu.VMEM((owners, 2, pad, splats), F32),
        pltpu.VMEM((depth, pixels, splats), F32),
        pltpu.VMEM((depth, pixels, 2 * splats), BF16),
        pltpu.VMEM((depth, pixels, splats), F32),
        pltpu.VMEM((pixels, splats), F32),
        pltpu.VMEM((2 * splats, 2 * splats), BF16),
        pltpu.VMEM((2 * splats, 2 * splats), BF16),
        pltpu.VMEM((16, pixels), BF16),
        pltpu.VMEM((pixels, 128), BF16),
        pltpu.VMEM((8, pixels), F32),
        dma((owned,)),
        dma((2, groups - 1)),
        dma((2, groups, 2, share)),
        dma((2, owners - 1)),
        dma((2, cameras, owners - 1)),
        dma((2, cameras, groups - 1, owners)),
        dma((2, owners - 1)),
        dma((owned,)),
        dma((owners,)),
        dma((3 + cameras,)),
    ]
    images, fresh, new_moments, children = pl.pallas_call(
        step_kernel,
        out_shape=(
            shape((cameras, 3, tiles, pixels), F32),
            shape((owned, pad, splats), F32),
            shape((2, share, pad, splats), F32),
            shape((owners, 2, pad, splats), F32),
        ),
        in_specs=[SMEM] * 5 + [VMEM] * 2 + [ANY] * 3,
        out_specs=(VMEM, ANY, ANY, ANY),
        scratch_shapes=scratch,
        compiler_params=pltpu.CompilerParams(
            collective_id=5, has_side_effects=True, vmem_limit_bytes=BIG
        ),
        name="step",
    )(
        send_block.transpose(0, 1, 3, 2), tile_slot, tile_count, split_block, split_live,
        targets.transpose(0, 2, 1, 3), cam_proj.transpose(1, 0, 2),
        params.transpose(1, 0, 2), by_value(moment_first), by_value(moment_second),
    )
    images, new_params, new_first, new_second, children = spread_out(
        images, fresh, new_moments, children, values
    )
    restore = lambda moment: moment.transpose(1, 0, 2).reshape(moment_first.shape)
    return (
        images.transpose(0, 2, 1, 3),
        new_params.transpose(1, 0, 2),
        restore(new_first),
        restore(new_second),
        children.transpose(0, 2, 1, 3),
    )


def solution(mesh):
    placed = (
        P("dev", None, None),
        P("dev", "cam", None, None, None),
        P("dev", "cam", None, None, None),
        P("cam", None, None),
        P("cam", "dev", None, None),
        P("cam", "dev", None),
        P("cam", "dev"),
        P("cam", "dev", None, None),
        P("dev", None),
        P("dev", None),
    )
    return jax.shard_map(
        body,
        mesh=mesh,
        in_specs=placed,
        out_specs=(
            P("cam", "dev", None, None),
            P("dev", None, None),
            P("dev", "cam", None, None, None),
            P("dev", "cam", None, None, None),
            P("dev", None, None, None),
        ),
        check_vma=False,
    )
```

time: 67.7 us -> 53.2 us (0.79)
  Pallas kernels: 59.6 us -> 52.1 us
  starting transfers between devices: 4.47 us -> 0 us
  other arithmetic: 2.47 us -> 0 us
    pallas_call x6 -> x2, Pallas kernels: 59.6 us -> 52.1 us  [the longest x1 47.6 us: body(): pl.pallas_call(step_kernel, out_shape=(shape((cameras, 3, tiles, pixels),...]
    ppermute x3 -> x0, starting transfers between devices: 4.47 us -> none  [body(): packs.append(lax.ppermute(pack, 'cam', pattern))]
    convert_element_type x2 -> x0, other arithmetic: 1.38 us -> none  [the longest x1 0.69 us: body(): numbers = send_block.astype(F32).reshape(-1)]
    concatenate x1 -> x0, other arithmetic: 1.1 us -> none  [body(): jnp.concatenate([by_value(moment_first), by_value(moment_second), matrix,...]
  transfers between devices with their start and end apart: 3 -> 0, of which waited for: 0 -> 0; matrix products, arithmetic and copies ran while one was open for 0% -> 0% of each run, Pallas kernels for 61% -> 0%
where the time goes in v1:
time: 53.2 us; the launch traced here: 52.8 us
  Pallas kernels  52.1 us (98%)
  between operations  0.64 us (1%)
    pallas_call x1, Pallas kernels, body(): pl.pallas_call(step_kernel, out_shape=(shape((cameras, 3, tiles, pixels),...  47.6 us
    pallas_call x1, Pallas kernels, spread_out(): pl.pallas_call(spread_kernel, out_shape=(shape(images.shape, F32), shape(...  4.52 us

profile of v1, /device:TPU:1, one launch (start us, length us, event | category | flops | bytes accessed | tf_op | source)
XLA Modules:
  0.0 52.8 jit_solution(15763093499415242158)
XLA Ops:
  0.6 47.6 %step.1 = (f32[2,3,2,256]{3,2,1,0:T(2,128)}, f32[32,64,128]{2,1,0:T(8,128)}, f32[2,8,64,128]{3,2,1,0:T(8,128)}, f32[8,2,64,128]{3,2,1,0:T(8,128)}) custom-call(s32[2,1,2,8]{3,2,1,0:T(2,128)} %bitcast.24, s32[2,2,8]{2,1,0:T(2,128)} %slot_ref.1, s32[2,2]{1,0:T(2,128)} %count_ref.1, s32[1,8]{1,0:T(1,128)} %split_ref.1, s32[1,8]{1,0:T(1,128)} %live_ref.1, ...), custom_call_target="tpu_custom_call" | custom-call | tf_op jit(solution)/shard_map/step/pallas_call | solution.py:765
  48.3 4.5 %spread.1 = (f32[2,3,2,256]{3,2,1,0:T(2,128)}, f32[59,32,128]{2,1,0:T(8,128)}, f32[59,8,128]{2,1,0:T(8,128)}, f32[59,8,128]{2,1,0:T(8,128)}, f32[8,59,2,128]{3,2,1,0:T(2,128)}) custom-call(f32[2,3,2,256]{3,2,1,0:T(2,128)} %get-tuple-element.14.image_ref, f32[32,64,128]{2,1,0:T(8,128)} %get-tuple-element.15.fresh_ref, ...), custom_call_target="tpu_custom_call" | custom-call | tf_op jit(solution)/shard_map/spread/pallas_call | solution.py:685

commit v2 on v1

--- a/solution.py
+++ b/solution.py
@@ -10,7 +10,7 @@
 
 TSIDE = 16
 PROJ = 9
-PAIR = 2
+PAIR = 4
 LOSS_WEIGHT = 256.0
 RATE = 0.01
 BETA_FIRST = 0.9
@@ -299,7 +299,7 @@
     send_ref, slot_ref, count_ref, split_ref, live_ref, target_ref, proj_ref,
     params_hbm, first_hbm, second_hbm,
     image_ref, params_out, moments_out, child_out,
-    meta, blocks, moments, parcels, raw, feats, saved, entries, back, gathered, table,
+    meta, blocks, moments, arrived, parcels, raw, feats, saved, entries, back, gathered, table,
     fresh, new_moments, parents, landed, children,
     weights, pairs, ratios, carry, before, after_tri, cot_rows, cot_cols, picture,
     load_sems, meta_sems, moment_sems, raw_sems, back_sems, cross_sems, parent_sems, out_sems,
@@ -406,23 +406,22 @@
                 meta_sems.at[0, turn - 1], meta_sems.at[1, turn - 1], "cam", peer_cam[turn],
             )
         )
-    for turn in range(1, groups):
-        for kind, source in enumerate((first_hbm, second_hbm)):
-            for place in range(share):
-                moment_copies.append(
-                    send(
-                        source.at[:, place, :],
-                        moments.at[kind, group * share + place, pl.ds(0, values), :],
-                        moment_sems.at[0, turn - 1, kind, place],
-                        moment_sems.at[1, turn - 1, kind, place],
-                        "cam", peer_cam[turn],
-                    )
-                )
+    near = [lax.rem(group, 2) * -2 + 1 + group, lax.rem(group + 2, groups)]
+    far = groups - 1 - group
+    for kind, source in enumerate((first_hbm, second_hbm)):
+        for side in range(2):
+            moment_copies.append(
+                send(
+                    source, arrived.at[group, kind],
+                    moment_sems.at[0, side, kind, 0], moment_sems.at[1, side, kind, 0],
+                    "cam", near[side],
+                )
+            )
     own_moments = [
         keep(
             source.at[:, place, :],
             moments.at[kind, group * share + place, pl.ds(0, values), :],
-            moment_sems.at[0, groups - 1, kind, place],
+            moment_sems.at[0, 0, kind, 1 + place],
         )
         for kind, source in enumerate((first_hbm, second_hbm))
         for place in range(share)
@@ -529,11 +528,40 @@
                     result[:, number * splats : (number + 1) * splats]
                 )
 
+    moment_moves = []
+
+    def settle(kind, origin, side):
+        for place in range(share):
+            moment_moves.append(
+                keep(
+                    arrived.at[origin, kind, :, place, :],
+                    moments.at[kind, origin * share + place, pl.ds(0, values), :],
+                    moment_sems.at[1, side, kind, 1 + place],
+                )
+            )
+
+    def pass_moments():
+        for kind in range(2):
+            for side in range(2):
+                moment_copies[kind * 2 + side].wait_recv()
+                origin = near[side]
+                if side == kind:
+                    moment_copies.append(
+                        send(
+                            arrived.at[origin, kind], arrived.at[origin, kind],
+                            moment_sems.at[0, 2, kind, 0], moment_sems.at[1, 2, kind, 0],
+                            "cam", near[1 - side],
+                        )
+                    )
+                settle(kind, origin, side)
+
     for camera in range(cameras):
         for tile in range(tiles):
             render(camera, tile)
             if camera and tile == 0:
                 send_across(camera - 1)
+        if camera == 0:
+            pass_moments()
         slot_sums(camera)
         send_back(camera)
     table[:, rows:high_rows, :] = jnp.zeros((owned, high_rows - rows, splats), F32)
@@ -553,9 +581,10 @@
             for step in range(owners):
                 cross_copies[camera][step * (groups - 1) + turn - 1].wait_recv()
             scatter(turn, camera)
-    for copy in moment_copies:
-        copy.wait_recv()
-    for copy in own_moments:
+    for kind in range(2):
+        moment_copies[4 + kind].wait_recv()
+        settle(kind, far, 2)
+    for copy in own_moments + moment_moves:
         copy.wait()
 
     def gradients(couple):
@@ -596,13 +625,20 @@
             new_moments[0, block] = new_first
             new_moments[1, block] = new_second
             outs.append(
-                keep(fresh.at[block], params_out.at[block], out_sems.at[block])
-            )
-    outs.append(
-        keep(
-            new_moments.at[:, pl.ds(group * share, share)], moments_out, own_sems.at[2 + cameras]
-        )
-    )
+                keep(
+                    fresh.at[block, pl.ds(0, values), :], params_out.at[:, block, :],
+                    out_sems.at[block],
+                )
+            )
+    for kind in range(2):
+        for place in range(share):
+            outs.append(
+                keep(
+                    new_moments.at[kind, group * share + place, pl.ds(0, values), :],
+                    moments_out.at[kind, :, place, :],
+                    moment_sems.at[0, 1, kind, 1 + place],
+                )
+            )
     for step in range(owners):
         source = from_dev[step]
         if step:
@@ -618,7 +654,14 @@
         shrunk = parent - jnp.where((line >= 3) & (line < 6), SHRINK, 0.0) * alive
         children[source, 0] = shrunk + shift
         children[source, 1] = shrunk - shift
-        outs.append(keep(children.at[source], child_out.at[source], child_sems.at[step]))
+        for kind in range(2):
+            outs.append(
+                keep(
+                    children.at[source, kind, pl.ds(0, values), :],
+                    child_out.at[source, :, kind, :],
+                    child_sems.at[kind, step],
+                )
+            )
     for copy in outs:
         copy.wait()
     for copy in raw_copies + meta_copies + moment_copies + parent_copies:
@@ -633,63 +676,41 @@
     image_out, params_out, first_out, second_out, child_out,
     fresh, moments, children, in_sems, out_sems,
 ):
-    owned = fresh.shape[0]
+    values = fresh.shape[0]
     owners = children.shape[0]
-    share = moments.shape[1]
-    values = params_out.shape[0]
-    lump = 8
-    loads, jobs = [], []
-    for start in range(0, owned, lump):
-        some = pl.ds(start, min(lump, owned - start))
-        loads.append((fresh_ref.at[some], fresh.at[some]))
-        jobs.append(
-            [
-                (fresh.at[block, pl.ds(0, values), :], params_out.at[:, block, :])
-                for block in range(start, min(start + lump, owned))
-            ]
-        )
-    for start in range(0, owners, lump):
-        some = pl.ds(start, min(lump, owners - start))
-        loads.append((children_ref.at[some], children.at[some]))
-        jobs.append(
-            [
-                (children.at[source, kind, pl.ds(0, values), :], child_out.at[source, :, kind, :])
-                for source in range(start, min(start + lump, owners))
-                for kind in range(2)
-            ]
-        )
+    trips = []
+    for start in range(0, values, 15):
+        some = pl.ds(start, min(15, values - start))
+        trips.append((fresh_ref.at[some], fresh.at[some], params_out.at[some]))
+    for start in range(0, owners, 4):
+        some = pl.ds(start, min(4, owners - start))
+        trips.append((children_ref.at[some], children.at[some], child_out.at[some]))
     for kind, target in enumerate((first_out, second_out)):
-        loads.append((moments_ref.at[kind], moments.at[kind]))
-        jobs.append(
-            [
-                (moments.at[kind, place, pl.ds(0, values), :], target.at[:, place, :])
-                for place in range(share)
-            ]
-        )
-    started = [keep(src, dst, in_sems.at[number]) for number, (src, dst) in enumerate(loads)]
+        trips.append((moments_ref.at[kind], moments.at[kind], target))
+    started = [keep(src, mid, in_sems.at[at]) for at, (src, mid, _) in enumerate(trips)]
     image_out[...] = image_ref[...]
     outs = []
-    for copy, job in zip(started, jobs):
-        copy.wait()
-        for src, dst in job:
-            outs.append(keep(src, dst, out_sems.at[len(outs)]))
+    for at, (_, mid, dst) in enumerate(trips):
+        started[at].wait()
+        outs.append(keep(mid, dst, out_sems.at[at]))
     for copy in outs:
         copy.wait()
 
 
-def spread_out(images, fresh, new_moments, children, values):
-    owned, pad, splats = fresh.shape
-    share = new_moments.shape[1]
+def spread_out(images, fresh, new_moments, children):
+    values, _, splats = fresh.shape
     owners = children.shape[0]
     shape = jax.ShapeDtypeStruct
+    moments = shape(new_moments.shape[1:], F32)
+    trips = -(-values // 15) + -(-owners // 4) + 2
     return pl.pallas_call(
         spread_kernel,
         out_shape=(
             shape(images.shape, F32),
-            shape((values, owned, splats), F32),
-            shape((values, share, splats), F32),
-            shape((values, share, splats), F32),
-            shape((owners, values, 2, splats), F32),
+            shape(fresh.shape, F32),
+            moments,
+            moments,
+            shape(children.shape, F32),
         ),
         in_specs=[VMEM, ANY, ANY, ANY],
         out_specs=(VMEM, ANY, ANY, ANY, ANY),
@@ -697,8 +718,8 @@
             pltpu.VMEM(fresh.shape, F32),
             pltpu.VMEM(new_moments.shape, F32),
             pltpu.VMEM(children.shape, F32),
-            pltpu.SemaphoreType.DMA((owned + owners + 2,)),
-            pltpu.SemaphoreType.DMA((owned + 2 * owners + 2 * share,)),
+            pltpu.SemaphoreType.DMA((trips,)),
+            pltpu.SemaphoreType.DMA((trips,)),
         ],
         compiler_params=pltpu.CompilerParams(vmem_limit_bytes=BIG),
         name="spread",
@@ -729,6 +750,7 @@
         pltpu.VMEM((groups, meta_rows, 128), F32),
         pltpu.VMEM((owned, pad, splats), F32),
         pltpu.VMEM((2, owned, pad, splats), F32),
+        pltpu.VMEM((groups, 2, values, share, splats), F32),
         pltpu.VMEM((owners, indices, 16, splats), F32),
         pltpu.VMEM((indices, PROJ, owners, splats), F32),
         pltpu.VMEM((indices * owners, 16, splats), F32),
@@ -753,22 +775,22 @@
         pltpu.VMEM((8, pixels), F32),
         dma((owned,)),
         dma((2, groups - 1)),
-        dma((2, groups, 2, share)),
+        dma((2, groups - 1, 2, 1 + share)),
         dma((2, owners - 1)),
         dma((2, cameras, owners - 1)),
         dma((2, cameras, groups - 1, owners)),
         dma((2, owners - 1)),
         dma((owned,)),
-        dma((owners,)),
-        dma((3 + cameras,)),
+        dma((2, owners)),
+        dma((2 + cameras,)),
     ]
     images, fresh, new_moments, children = pl.pallas_call(
         step_kernel,
         out_shape=(
             shape((cameras, 3, tiles, pixels), F32),
-            shape((owned, pad, splats), F32),
-            shape((2, share, pad, splats), F32),
-            shape((owners, 2, pad, splats), F32),
+            shape((values, owned, splats), F32),
+            shape((2, values, share, splats), F32),
+            shape((owners, values, 2, splats), F32),
         ),
         in_specs=[SMEM] * 5 + [VMEM] * 2 + [ANY] * 3,
         out_specs=(VMEM, ANY, ANY, ANY),
@@ -783,7 +805,7 @@
         params.transpose(1, 0, 2), by_value(moment_first), by_value(moment_second),
     )
     images, new_params, new_first, new_second, children = spread_out(
-        images, fresh, new_moments, children, values
+        images, fresh, new_moments, children
     )
     restore = lambda moment: moment.transpose(1, 0, 2).reshape(moment_first.shape)
     return (

time: 53.2 us -> 50 us (0.940)
  Pallas kernels: 52.1 us -> 49 us
    pallas_call x1, Pallas kernels: 47.6 us -> 45.2 us  [body(): pl.pallas_call(step_kernel, out_shape=(shape((cameras, 3, tiles, pixels),...]
    pallas_call x1, Pallas kernels: 4.52 us -> 3.76 us  [spread_out(): pl.pallas_call(spread_kernel, out_shape=(shape(images.shape, F32), shape(...]
where the time goes in v2:
time: 50 us; the launch traced here: 49.6 us
  Pallas kernels  49 us (98%)
  between operations  0.64 us (1%)
    pallas_call x1, Pallas kernels, body(): pl.pallas_call(step_kernel, out_shape=(shape((cameras, 3, tiles, pixels),...  45.2 us
    pallas_call x1, Pallas kernels, spread_out(): pl.pallas_call(spread_kernel, out_shape=(shape(images.shape, F32), shape(...  3.76 us

profile of v2, /device:TPU:1, one launch (start us, length us, event | category | flops | bytes accessed | tf_op | source)
XLA Modules:
  0.0 49.6 jit_solution(2558491839515367506)
XLA Ops:
  0.6 45.2 %step.1 = (f32[2,3,2,256]{3,2,1,0:T(2,128)}, f32[59,32,128]{2,1,0:T(8,128)}, f32[2,59,8,128]{3,2,1,0:T(8,128)}, f32[8,59,2,128]{3,2,1,0:T(2,128)}) custom-call(s32[2,1,2,8]{3,2,1,0:T(2,128)} %bitcast.24, s32[2,2,8]{2,1,0:T(2,128)} %slot_ref.1, s32[2,2]{1,0:T(2,128)} %count_ref.1, s32[1,8]{1,0:T(1,128)} %split_ref.1, s32[1,8]{1,0:T(1,128)} %live_ref.1, ...), custom_call_target="tpu_custom_call" | custom-call | tf_op jit(solution)/shard_map/step/pallas_call | solution.py:787
  45.9 3.8 %spread.1 = (f32[2,3,2,256]{3,2,1,0:T(2,128)}, f32[59,32,128]{2,1,0:T(8,128)}, f32[59,8,128]{2,1,0:T(8,128)}, f32[59,8,128]{2,1,0:T(8,128)}, f32[8,59,2,128]{3,2,1,0:T(2,128)}) custom-call(f32[2,3,2,256]{3,2,1,0:T(2,128)} %get-tuple-element.14.image_ref, f32[59,32,128]{2,1,0:T(8,128)} %get-tuple-element.15.fresh_ref, ...), custom_call_target="tpu_custom_call" | custom-call | tf_op jit(solution)/shard_map/spread/pallas_call | solution.py:706
